TPU v7x, 256 devices: a whole 4x4x8 slice. The times are simulated.
256 devices in a mesh: gx: 8 (over x, core), gy: 8 (over z), gz: 4 (over y).
Axes of the slice: x: 4, y: 4, z: 8, core: 2. Of those that a mesh axis runs over, the one named last changes fastest.
Arguments:
- load_field: float32 [3, 128, 128, 512], P(None, 'gx', 'gy', 'gz'), may hold values from -6 to 6
- design: float32 [128, 128, 512], P('gx', 'gy', 'gz'), may hold values from 0 to 1
- solid_map: int32 [8, 8, 32], replicated, may hold values from 0 to 1, as said below
Outputs:
- displacement: float32 [3, 128, 128, 512], P(None, 'gx', 'gy', 'gz')
- sensitivity: float32 [128, 128, 512], P('gx', 'gy', 'gz')
- density: float32 [128, 128, 512], P('gx', 'gy', 'gz')
Inputs may be any that keep to these rules, and one draw needn't show every extreme that they name: Brick [i, j, k] holds the elements of rows i * 16 to (i + 1) * 16 - 1 of each dimension in turn. For i < 4, every j and every aligned run of 8 bricks along the third dimension, the run at first index i and the same run at i + 4 hold exactly 8 solid bricks together. The run solid_map[0, 0, 0:8] is all solid.
All inputs are finite; a program needn't handle non-finite values.
Results may differ from a plain program's by a relative error of at most 0.0001.
Values sent between devices are 32-bit elements; how exact they have to be, the bound alone decides.
No kernel may reach another device: no remote copies, remote signals or barrier semaphores. Data moves between devices by JAX's collectives and lax.ppermute only.
A program may use at most 64 MiB of HBM per device.

v0:
```python
import math
import jax
import jax.numpy as jnp
import numpy as np
from jax import lax
from jax.sharding import Mesh
from jax.sharding import PartitionSpec as P

BRICK = 16
ITERS = 2
GX = ("gx_0", "gx_1")
GX_GY_GZ = ("gx_0", "gx_1", "gy", "gz")
young_floor = 0.001
spring_rate = 0.05
sharpness = 8.0
threshold = 0.5
poisson = 0.3
precise = lax.Precision.HIGHEST


def with_halo(block, sides, width):
    for axis, dim in sides:
        count = lax.axis_size(axis)
        forward = [(i, i + 1) for i in range(count - 1)]
        backward = [(target, source) for source, target in forward]
        low = lax.ppermute(
            lax.slice_in_dim(block, block.shape[dim] - width, None, axis=dim), axis, forward
        )
        high = lax.ppermute(lax.slice_in_dim(block, 0, width, axis=dim), axis, backward)
        block = jnp.concatenate([low, block, high], axis=dim)
    return block


def shifted(block, axis, distance):
    devices = range(lax.axis_size(axis))
    route = [(i - distance, i) for i in devices if i - distance in devices]
    return lax.ppermute(block, axis, route)


def over_axes(value, axes):
    for axis in axes:
        value = lax.psum(value, axis)
    return value


def element_matrix():
    lame_first = poisson / ((1.0 + poisson) * (1.0 - 2.0 * poisson))
    shear_mod = 1.0 / (2.0 * (1.0 + poisson))
    elastic = np.zeros((6, 6))
    elastic[:3, :3] = lame_first
    for axis_one in range(3):
        elastic[axis_one, axis_one] += 2.0 * shear_mod
        elastic[axis_one + 3, axis_one + 3] = shear_mod
    gauss_point = 1.0 / math.sqrt(3.0)
    stiffness = np.zeros((24, 24))
    for point_x in (-gauss_point, gauss_point):
        for point_y in (-gauss_point, gauss_point):
            for point_z in (-gauss_point, gauss_point):
                strain = np.zeros((6, 24))
                for corner in range(8):
                    sign_a = 2 * (corner // 4) - 1
                    sign_b = 2 * (corner // 2 % 2) - 1
                    sign_c = 2 * (corner % 2) - 1
                    along_x = 0.25 * sign_a * (1 + sign_b * point_y) * (1 + sign_c * point_z)
                    along_y = 0.25 * (1 + sign_a * point_x) * sign_b * (1 + sign_c * point_z)
                    along_z = 0.25 * (1 + sign_a * point_x) * (1 + sign_b * point_y) * sign_c
                    column = 3 * corner
                    strain[0, column] = along_x
                    strain[1, column + 1] = along_y
                    strain[2, column + 2] = along_z
                    strain[3, column + 1] = along_z
                    strain[3, column + 2] = along_y
                    strain[4, column] = along_z
                    strain[4, column + 2] = along_x
                    strain[5, column] = along_y
                    strain[5, column + 1] = along_x
                stiffness += strain.T @ elastic @ strain * 0.125
    return jnp.asarray(stiffness, dtype=jnp.float32)


def cone_offsets():
    listed = []
    for step_x in range(-2, 3):
        for step_y in range(-2, 3):
            for step_z in range(-2, 3):
                radius = step_x * step_x + step_y * step_y + step_z * step_z
                if radius < 9:
                    listed.append((step_x, step_y, step_z, 3.0 - math.sqrt(radius)))
    return listed


def corner_values(node_values, width_x, width_y, width_z):
    pieces = []
    for corner in range(8):
        shift_a, shift_b, shift_c = (corner // 4, corner // 2 % 2, corner % 2)
        pieces.append(
            node_values[
                :,
                shift_a : shift_a + width_x,
                shift_b : shift_b + width_y,
                shift_c : shift_c + width_z,
            ]
        )
    return jnp.concatenate(pieces, 0).reshape(24, -1)


def spread_back(forces, width_x, width_y, width_z):
    forces = forces.reshape(24, width_x, width_y, width_z)
    summed = jnp.zeros((3, width_x + 1, width_y + 1, width_z + 1), jnp.float32)
    for corner in range(8):
        shift_a, shift_b, shift_c = (corner // 4, corner // 2 % 2, corner % 2)
        summed = summed + jnp.pad(
            forces[3 * corner : 3 * corner + 3],
            ((0, 0), (shift_a, 1 - shift_a), (shift_b, 1 - shift_b), (shift_c, 1 - shift_c)),
        )
    return summed


def corner_energy(stiffness, corner_vals):
    return jnp.sum(
        corner_vals
        * jnp.dot(stiffness, corner_vals, precision=precise, preferred_element_type=jnp.float32),
        0,
    )


def brick_product(stiffness, node_values, brick_moduli):
    width_x, width_y, width_z = brick_moduli.shape
    corner_vals = corner_values(node_values, width_x, width_y, width_z)
    forces = jnp.dot(
        stiffness,
        corner_vals * brick_moduli.reshape(1, -1),
        precision=precise,
        preferred_element_type=jnp.float32,
    )
    return spread_back(forces, width_x, width_y, width_z)


def body(load_field, design, solid_map):
    stiffness = element_matrix()
    offsets = cone_offsets()
    size_x, size_y, size_z = design.shape
    bricks_here = size_z // BRICK
    devices_x = lax.axis_size(GX)
    index_x = lax.axis_index(GX)
    index_y = lax.axis_index("gy")
    index_z = lax.axis_index("gz")

    def inside(dev_index, length, devices):
        coords = dev_index * length + jnp.arange(length, dtype=jnp.int32)
        return {
            step_off: ((coords + step_off >= 0) & (coords + step_off < length * devices)).astype(
                jnp.float32
            )
            for step_off in range(-2, 3)
        }

    inside_x = inside(index_x, size_x, devices_x)
    inside_y = inside(index_y, size_y, lax.axis_size("gy"))
    inside_z = inside(index_z, size_z, lax.axis_size("gz"))
    weight_sum = jnp.zeros((size_x, size_y, size_z), jnp.float32)
    for step_x, step_y, step_z, weight in offsets:
        weight_sum = weight_sum + weight * (
            inside_x[step_x][:, None, None]
            * inside_y[step_y][None, :, None]
            * inside_z[step_z][None, None, :]
        )

    def cone_sum(values):
        extended = with_halo(values, ((GX, 0), ("gy", 1), ("gz", 2)), 2)
        summed = jnp.zeros_like(values)
        for step_x, step_y, step_z, weight in offsets:
            summed = (
                summed
                + weight
                * extended[
                    2 + step_x : 2 + step_x + size_x,
                    2 + step_y : 2 + step_y + size_y,
                    2 + step_z : 2 + step_z + size_z,
                ]
            )
        return summed

    smoothed = cone_sum(design) / weight_sum
    lift_value = math.tanh(sharpness * threshold)
    scale_sum = lift_value + math.tanh(sharpness * (1.0 - threshold))
    tanh_shift = jnp.tanh(sharpness * (smoothed - threshold))
    density = (lift_value + tanh_shift) / scale_sum
    own_flags = lax.dynamic_slice(
        solid_map, (index_x, index_y, index_z * bricks_here), (1, 1, bricks_here)
    ).reshape(bricks_here)
    cell_flags = jnp.repeat(own_flags.astype(jnp.float32), BRICK)
    moduli = (young_floor + density**3 * (1.0 - young_floor)) * cell_flags

    def clamp_axis(length, devices, dev_index):
        return jnp.where(
            (jnp.arange(length + 1) == length) & (dev_index == devices - 1), 0.0, 1.0
        ).astype(jnp.float32)

    clamp_mask = (
        clamp_axis(size_x, devices_x, index_x)[:, None, None]
        * clamp_axis(size_y, lax.axis_size("gy"), index_y)[None, :, None]
        * clamp_axis(size_z, lax.axis_size("gz"), index_z)[None, None, :]
    )

    def assemble(partial_value):
        extended = with_halo(partial_value, ((GX, 1), ("gy", 2), ("gz", 3)), 1)
        for axis_one in (1, 2, 3):
            length = extended.shape[axis_one]
            lower_part = lax.slice_in_dim(extended, 0, 1, axis=axis_one) + lax.slice_in_dim(
                extended, 1, 2, axis=axis_one
            )
            middle = lax.slice_in_dim(extended, 2, length - 2, axis=axis_one)
            upper_part = lax.slice_in_dim(
                extended, length - 2, length - 1, axis=axis_one
            ) + lax.slice_in_dim(extended, length - 1, length, axis=axis_one)
            extended = jnp.concatenate([lower_part, middle, upper_part], axis_one)
        return extended * clamp_mask

    def owned_sum(left, right):
        return jnp.sum(left[:, :size_x, :size_y, :size_z] * right[:, :size_x, :size_y, :size_z])

    zero_nodes = jnp.zeros((3, size_x + 1, size_y + 1, size_z + 1), jnp.float32)

    def piece_of(node_values, offset_z):
        return lax.dynamic_slice_in_dim(node_values, offset_z, BRICK + 1, 3)

    def moduli_of(offset_z):
        return lax.dynamic_slice_in_dim(moduli, offset_z, BRICK, 2)

    def add_into(summed, offset_z, contribution):
        current = lax.dynamic_slice_in_dim(summed, offset_z, BRICK + 1, 3)
        return lax.dynamic_update_slice_in_dim(summed, current + contribution, offset_z, 3)

    def products(node_values):

        def brick_step(position, summed):
            offset_z = position * BRICK

            def brick_compute(summed):
                return add_into(
                    summed,
                    offset_z,
                    brick_product(stiffness, piece_of(node_values, offset_z), moduli_of(offset_z)),
                )

            def skip_brick(summed):
                return summed

            return lax.cond(own_flags[position] > 0, brick_compute, skip_brick, summed)

        return lax.fori_loop(0, bricks_here, brick_step, zero_nodes)

    def operate(vector):
        return assemble(products(vector)) + spring_rate * vector

    upper_z = shifted(load_field[:, :, :, :1], "gz", -1)
    extended_z = jnp.concatenate([load_field, upper_z], 3)
    upper_y = shifted(extended_z[:, :, :1, :], "gy", -1)
    extended_y = jnp.concatenate([extended_z, upper_y], 2)
    upper_x = shifted(extended_y[:, :1, :, :], GX, -1)
    loaded = jnp.concatenate([extended_y, upper_x], 1) * clamp_mask

    def two_products(residual, applied):
        return (
            over_axes(owned_sum(residual, residual), GX_GY_GZ),
            over_axes(owned_sum(residual, applied), GX_GY_GZ),
        )

    solution = zero_nodes
    residual = loaded
    applied = operate(residual)
    norm_now, product = two_products(residual, applied)
    step_size = norm_now / product
    direction, applied_dir = (residual, applied)
    for iteration in range(ITERS):
        solution = solution + step_size * direction
        residual = residual - step_size * applied_dir
        if iteration + 1 < ITERS:
            applied = operate(residual)
            norm_next, product = two_products(residual, applied)
            norm_ratio = norm_next / norm_now
            step_size = norm_next / (product - norm_ratio * norm_next / step_size)
            direction = residual + norm_ratio * direction
            applied_dir = applied + norm_ratio * applied_dir
            norm_now = norm_next

    def energy_step(position, summed):
        offset_z = position * BRICK

        def energy_compute(summed):
            corner_vals = corner_values(piece_of(solution, offset_z), size_x, size_y, BRICK)
            values = corner_energy(stiffness, corner_vals).reshape(size_x, size_y, BRICK)
            return lax.dynamic_update_slice_in_dim(summed, values, offset_z, 2)

        def skip_energy(summed):
            return summed

        return lax.cond(own_flags[position] > 0, energy_compute, skip_energy, summed)

    energy = lax.fori_loop(
        0, bricks_here, energy_step, jnp.zeros((size_x, size_y, size_z), jnp.float32)
    )
    pushed = (
        -3.0
        * (1.0 - young_floor)
        * density**2
        * cell_flags
        * energy
        * (sharpness * (1.0 - tanh_shift * tanh_shift) / scale_sum)
        / weight_sum
    )
    sensitivity = cone_sum(pushed)
    return (solution[:, :size_x, :size_y, :size_z], sensitivity, density)


def solution(mesh):
    torus = Mesh(
        mesh.devices.reshape(4, 2, mesh.shape["gy"], mesh.shape["gz"]), ("gx_0", "gx_1", "gy", "gz")
    )
    placed = (P(None, GX, "gy", "gz"), P(GX, "gy", "gz"), P())
    return jax.shard_map(
        body,
        mesh=torus,
        in_specs=placed,
        out_specs=(P(None, GX, "gy", "gz"), P(GX, "gy", "gz"), P(GX, "gy", "gz")),
        check_vma=False,
    )
```

profile of v0, /device:TPU:1, one launch (start us, length us, event | category | flops | bytes accessed | tf_op | source)
XLA Modules:
  0.0 896.5 jit_solution(13874755931423796651)
XLA Ops:
  12.2 8.4 collective-permute-done
  48.3 46.9 %while.51 = (s32[]{:T(128)}, f32[3,17,17,129]{3,2,1,0:T(8,128)}, s32[8]{0:T(128)}, f32[3,17,17,129]{3,2,1,0:T(8,128)S(1)}, f32[16,16,128]{2,1,0:T(8,128)}, /*index=5*/s32[]{:T(128)}, s32[1]{0:T(128)}) while((s32[]{:T(128)}, f32[3,17,17,129]{3,2,1,0:T(8,128)}, s32[8]{0:T(128)}, f32[3,17,17,129]{3,2,1,0:T(8,128)S(1)}, ...), condition=%wide.region_8.9_spmd.clone, body=%wide.region_5.8_spmd.sunk.clone.sunk | while | flops 28527780 | bytes 7407486 | solution.py:252
  56.1 31.4 %conditional.12 = (f32[3,17,17,129]{3,2,1,0:T(8,128)}) conditional(s32[]{:T(128)} %bitcast.33, f32[3,17,17,129]{3,2,1,0:T(8,128)} %get-tuple-element.762, (s32[]{:T(128)}, f32[3,17,17,129]{3,2,1,0:T(8,128)}, f32[3,17,17,129]{3,2,1,0:T(8,128)S(1)}, f32[16,16,128]{2,1,0:T(8,128)}) %tuple.222), branch_computations={%region_6.6_spmd, %region_7.7_spmd.clone} | conditional | flops 28527776 | bytes 7407351 | solution.py:250
  76.0 11.5 %dynamic_update_slice.12 = f32[3,17,17,129]{3,2,1,0:T(8,128)} dynamic-update-slice(f32[3,17,17,129]{3,2,1,0:T(8,128)} %get-tuple-element.486, f32[3,17,17,17]{3,2,1,0:T(8,128)S(1)} %add_add_fusion, s32[]{:T(128)} %constant.166.clone.1, s32[]{:T(128)} %constant.166.clone.1, s32[]{:T(128)} %constant.166.clone.1, s32[]{:T(128)S(6)} %select_n.81) | dynamic-update-slice | bytes 117916 | tf_op jit(solution)/shard_map/while/body/eval_jaxpr/cond/branch_1_fun/dynamic_update_slice | solution.py:233
  96.2 163.3 %collective-permute-start.9 = (f32[3,1,17,129]{3,2,1,0:T(8,128)S(1)}, f32[3,1,17,129]{3,2,1,0:T(8,128)S(1)}, u32[]{:S(2)}, u32[]{:S(2)}) collective-permute-start(f32[3,1,17,129]{3,2,1,0:T(8,128)S(1)} %get-tuple-element.599), channel_id=1, source_target_pairs={{0,32},{32,64},{64,96},{96,128},{128,160},{160,192},{192,224},{1,3... | collective-permute-start | bytes 78956 | tf_op jit(solution)/shard_map/ppermute | solution.py:26
  259.4 54.8 %collective-permute-start.10 = (f32[3,1,17,129]{3,2,1,0:T(8,128)S(1)}, f32[3,1,17,129]{3,2,1,0:T(8,128)S(1)}, u32[]{:S(2)}, u32[]{:S(2)}) collective-permute-start(f32[3,1,17,129]{3,2,1,0:T(8,128)S(1)} %get-tuple-element.600), channel_id=1, source_target_pairs={{32,0},{64,32},{96,64},{128,96},{160,128},{192,160},{224,192},{33,... | collective-permute-start | bytes 78956 | tf_op jit(solution)/shard_map/ppermute | solution.py:29
  326.3 11.0 %collective-permute-start.13 = (f32[3,19,19,1]{2,1,3,0:T(8,128)S(1)}, f32[3,19,19,1]{2,1,3,0:T(8,128)S(1)}, u32[]{:S(2)}, u32[]{:S(2)}) collective-permute-start(f32[3,19,19,1]{2,1,3,0:T(8,128)S(1)} %copy.48), channel_id=1, source_target_pairs={{0,1},{1,2},{2,3},{4,5},{5,6},{6,7},{8,9},{9,10},{10,11},{12,13},{... | collective-permute-start | bytes 13004 | tf_op jit(solution)/shard_map/ppermute | solution.py:26
  351.6 6.7 all-reduce.21
  358.3 7.5 all-reduce.23
  365.7 13.1 %all-reduce.17 = (f32[]{:T(128)}, f32[]{:T(128)}) all-reduce(f32[]{:T(128)} %get-tuple-element.554, f32[]{:T(128)} %get-tuple-element.555), channel_id=1, replica_groups=mesh['gx_0'=4,'gx_1'=2,'gy'=8,'gz'=4] {'gy'}, use_global_device_ids=true, to_apply=%region_3.4 | all-reduce | flops 2 | bytes 16 | tf_op jit(solution)/shard_map/psum | solution.py:42
  378.8 6.7 all-reduce.19
  389.3 46.8 %while.52 = (s32[]{:T(128)}, f32[3,17,17,129]{3,2,1,0:T(8,128)}, s32[8]{0:T(128)}, f32[3,17,17,129]{3,2,1,0:T(8,128)S(1)}, f32[16,16,128]{2,1,0:T(8,128)}, /*index=5*/s32[]{:T(128)}, s32[1]{0:T(128)}) while((s32[]{:T(128)}, f32[3,17,17,129]{3,2,1,0:T(8,128)}, s32[8]{0:T(128)}, f32[3,17,17,129]{3,2,1,0:T(8,128)S(1)}, ...), condition=%wide.region_22.23_spmd.clone, body=%wide.region_19.22_spmd.sunk.clone.sunk | while | flops 28527780 | bytes 7407486 | solution.py:252
  397.1 31.3 %conditional.13 = (f32[3,17,17,129]{3,2,1,0:T(8,128)}) conditional(s32[]{:T(128)} %bitcast.34, f32[3,17,17,129]{3,2,1,0:T(8,128)} %get-tuple-element.783, (s32[]{:T(128)}, f32[3,17,17,129]{3,2,1,0:T(8,128)}, f32[3,17,17,129]{3,2,1,0:T(8,128)S(1)}, f32[16,16,128]{2,1,0:T(8,128)}) %tuple.224), branch_computations={%region_20.20_spmd, %region_21.21_spmd.clone} | conditional | flops 28527776 | bytes 7407351 | solution.py:250
  416.9 11.5 %dynamic_update_slice.13 = f32[3,17,17,129]{3,2,1,0:T(8,128)} dynamic-update-slice(f32[3,17,17,129]{3,2,1,0:T(8,128)} %get-tuple-element.494, f32[3,17,17,17]{3,2,1,0:T(8,128)S(1)} %add_add_fusion.1, s32[]{:T(128)} %constant.174.clone.1, s32[]{:T(128)} %constant.174.clone.1, s32[]{:T(128)} %constant.174.clone.1, s32[]{:T(128)S(6)} %select_n.83) | dynamic-update-slice | bytes 117916 | tf_op jit(solution)/shard_map/while/body/eval_jaxpr/cond/branch_1_fun/dynamic_update_slice | solution.py:233
  437.1 165.1 %collective-permute-start.15 = (f32[3,1,17,129]{3,2,1,0:T(8,128)S(1)}, f32[3,1,17,129]{3,2,1,0:T(8,128)S(1)}, u32[]{:S(2)}, u32[]{:S(2)}) collective-permute-start(f32[3,1,17,129]{3,2,1,0:T(8,128)S(1)} %get-tuple-element.593), channel_id=1, source_target_pairs={{0,32},{32,64},{64,96},{96,128},{128,160},{160,192},{192,224},{1,3... | collective-permute-start | bytes 78956 | tf_op jit(solution)/shard_map/ppermute | solution.py:26
  602.2 56.5 %collective-permute-start.16 = (f32[3,1,17,129]{3,2,1,0:T(8,128)S(1)}, f32[3,1,17,129]{3,2,1,0:T(8,128)S(1)}, u32[]{:S(2)}, u32[]{:S(2)}) collective-permute-start(f32[3,1,17,129]{3,2,1,0:T(8,128)S(1)} %get-tuple-element.594), channel_id=1, source_target_pairs={{32,0},{64,32},{96,64},{128,96},{160,128},{192,160},{224,192},{33,... | collective-permute-start | bytes 78956 | tf_op jit(solution)/shard_map/ppermute | solution.py:29
  689.0 7.7 all-reduce.20
  696.7 6.8 all-reduce.22
  703.6 12.5 %all-reduce.16 = (f32[]{:T(128)}, f32[]{:T(128)}) all-reduce(f32[]{:T(128)} %get-tuple-element.552, f32[]{:T(128)} %get-tuple-element.553), channel_id=1, replica_groups=mesh['gx_0'=4,'gx_1'=2,'gy'=8,'gz'=4] {'gy'}, use_global_device_ids=true, to_apply=%region_17.18 | all-reduce | flops 2 | bytes 16 | tf_op jit(solution)/shard_map/psum | solution.py:42
  716.1 8.9 all-reduce.18
  731.3 29.9 %while.53 = (s32[]{:T(128)}, f32[16,16,128]{2,1,0:T(8,128)S(1)}, s32[8]{0:T(128)}, f32[3,17,17,129]{3,2,1,0:T(8,128)S(1)}, s32[]{:T(128)}, /*index=5*/s32[1]{0:T(128)}) while((s32[]{:T(128)}, f32[16,16,128]{2,1,0:T(8,128)S(1)}, s32[8]{0:T(128)}, f32[3,17,17,129]{3,2,1,0:T(8,128)S(1)}, s32[]{:T(128)}, ...), condition=%wide.region_32.33_spmd.clone, body=%wide.region_28.32_spmd.sunk.clone.sunk | while | flops 28504076 | bytes 4812342 | solution.py:301
  739.1 14.4 %conditional.14 = (f32[16,16,128]{2,1,0:T(8,128)S(1)}) conditional(s32[]{:T(128)} %bitcast.35, f32[16,16,128]{2,1,0:T(8,128)S(1)} %get-tuple-element.803, (s32[]{:T(128)}, f32[3,17,17,129]{3,2,1,0:T(8,128)S(1)}, f32[16,16,128]{2,1,0:T(8,128)S(1)}) %tuple.226), branch_computations={%region_29.29_spmd, %region_30.31_spmd.clone} | conditional | flops 28504072 | bytes 4812223 | solution.py:299
  763.2 81.2 %collective-permute-start.21 = (f32[2,16,128]{2,1,0:T(8,128)S(1)}, f32[2,16,128]{2,1,0:T(8,128)S(1)}, u32[]{:S(2)}, u32[]{:S(2)}) collective-permute-start(f32[2,16,128]{2,1,0:T(8,128)S(1)} %get-tuple-element.615), channel_id=1, source_target_pairs={{0,32},{32,64},{64,96},{96,128},{128,160},{160,192},{192,224},{1,3... | collective-permute-start | bytes 49160 | tf_op jit(solution)/shard_map/ppermute | solution.py:26
  844.4 26.2 %collective-permute-start.22 = (f32[2,16,128]{2,1,0:T(8,128)S(1)}, f32[2,16,128]{2,1,0:T(8,128)S(1)}, u32[]{:S(2)}, u32[]{:S(2)}) collective-permute-start(f32[2,16,128]{2,1,0:T(8,128)S(1)} %get-tuple-element.616), channel_id=1, source_target_pairs={{32,0},{64,32},{96,64},{128,96},{160,128},{192,160},{224,192},{33,... | collective-permute-start | bytes 49160 | tf_op jit(solution)/shard_map/ppermute | solution.py:29
  (378 shorter events, 211.9 us)
Async XLA Ops:
  1.4 20.7 %collective-permute-start.3 = (f32[2,16,128]{2,1,0:T(8,128)S(1)}, f32[2,16,128]{2,1,0:T(8,128)S(1)}, u32[]{:S(2)}, u32[]{:S(2)}) collective-permute-start(f32[2,16,128]{2,1,0:T(8,128)S(1)} %get-tuple-element.621), channel_id=1, source_target_pairs={{0,32},{32,64},{64,96},{96,128},{128,160},{160,192},{192,224},{1,3... | collective-permute-start | bytes 49160 | tf_op jit(solution)/shard_map/ppermute | solution.py:26
  5.9 16.3 %collective-permute-start.4 = (f32[2,16,128]{2,1,0:T(8,128)S(1)}, f32[2,16,128]{2,1,0:T(8,128)S(1)}, u32[]{:S(2)}, u32[]{:S(2)}) collective-permute-start(f32[2,16,128]{2,1,0:T(8,128)S(1)} %get-tuple-element.620), channel_id=1, source_target_pairs={{32,0},{64,32},{96,64},{128,96},{160,128},{192,160},{224,192},{33,... | collective-permute-start | bytes 49160 | tf_op jit(solution)/shard_map/ppermute | solution.py:29
  7.8 12.9 %collective-permute-start = (f32[3,16,16,1]{3,2,1,0:T(8,128)}, f32[3,16,16,1]{3,2,1,0:T(8,128)S(1)}, u32[]{:S(2)}, u32[]{:S(2)}) collective-permute-start(f32[3,16,16,1]{3,2,1,0:T(8,128)} %bitcast.36), channel_id=1, source_target_pairs={{1,0},{2,1},{3,2},{5,4},{6,5},{7,6},{9,8},{10,9},{11,10},{13,12},{... | collective-permute-start | bytes 9224 | tf_op jit(solution)/shard_map/ppermute | solution.py:37
  20.8 6.9 collective-permute-start.1
  22.2 5.5 collective-permute-start.5
  26.2 4.5 collective-permute-start.6
  30.9 6.9 collective-permute-start.7
  33.1 8.2 collective-permute-start.8
  34.4 12.1 %collective-permute-start.2 = (f32[3,1,17,129]{3,2,1,0:T(8,128)S(1)}, f32[3,1,17,129]{3,2,1,0:T(8,128)S(1)}, u32[]{:S(2)}, u32[]{:S(2)}) collective-permute-start(f32[3,1,17,129]{3,2,1,0:T(8,128)S(1)} %pad_maximum_fusion.25), channel_id=1, source_target_pairs={{32,0},{64,32},{96,64},{128,96},{160,128},{192,160},{224,192},{33,... | collective-permute-start | bytes 78956 | tf_op jit(solution)/shard_map/ppermute | solution.py:37
  96.2 219.7 %collective-permute-start.9 = (f32[3,1,17,129]{3,2,1,0:T(8,128)S(1)}, f32[3,1,17,129]{3,2,1,0:T(8,128)S(1)}, u32[]{:S(2)}, u32[]{:S(2)}) collective-permute-start(f32[3,1,17,129]{3,2,1,0:T(8,128)S(1)} %get-tuple-element.599), channel_id=1, source_target_pairs={{0,32},{32,64},{64,96},{96,128},{128,160},{160,192},{192,224},{1,3... | collective-permute-start | bytes 78956 | tf_op jit(solution)/shard_map/ppermute | solution.py:26
  259.4 56.5 %collective-permute-start.10 = (f32[3,1,17,129]{3,2,1,0:T(8,128)S(1)}, f32[3,1,17,129]{3,2,1,0:T(8,128)S(1)}, u32[]{:S(2)}, u32[]{:S(2)}) collective-permute-start(f32[3,1,17,129]{3,2,1,0:T(8,128)S(1)} %get-tuple-element.600), channel_id=1, source_target_pairs={{32,0},{64,32},{96,64},{128,96},{160,128},{192,160},{224,192},{33,... | collective-permute-start | bytes 78956 | tf_op jit(solution)/shard_map/ppermute | solution.py:29
  317.3 6.2 collective-permute-start.12
  326.3 14.9 %collective-permute-start.13 = (f32[3,19,19,1]{2,1,3,0:T(8,128)S(1)}, f32[3,19,19,1]{2,1,3,0:T(8,128)S(1)}, u32[]{:S(2)}, u32[]{:S(2)}) collective-permute-start(f32[3,19,19,1]{2,1,3,0:T(8,128)S(1)} %copy.48), channel_id=1, source_target_pairs={{0,1},{1,2},{2,3},{4,5},{5,6},{6,7},{8,9},{9,10},{10,11},{12,13},{... | collective-permute-start | bytes 13004 | tf_op jit(solution)/shard_map/ppermute | solution.py:26
  338.5 5.0 collective-permute-start.14
  437.1 223.2 %collective-permute-start.15 = (f32[3,1,17,129]{3,2,1,0:T(8,128)S(1)}, f32[3,1,17,129]{3,2,1,0:T(8,128)S(1)}, u32[]{:S(2)}, u32[]{:S(2)}) collective-permute-start(f32[3,1,17,129]{3,2,1,0:T(8,128)S(1)} %get-tuple-element.593), channel_id=1, source_target_pairs={{0,32},{32,64},{64,96},{96,128},{128,160},{160,192},{192,224},{1,3... | collective-permute-start | bytes 78956 | tf_op jit(solution)/shard_map/ppermute | solution.py:26
  602.2 58.2 %collective-permute-start.16 = (f32[3,1,17,129]{3,2,1,0:T(8,128)S(1)}, f32[3,1,17,129]{3,2,1,0:T(8,128)S(1)}, u32[]{:S(2)}, u32[]{:S(2)}) collective-permute-start(f32[3,1,17,129]{3,2,1,0:T(8,128)S(1)} %get-tuple-element.594), channel_id=1, source_target_pairs={{32,0},{64,32},{96,64},{128,96},{160,128},{192,160},{224,192},{33,... | collective-permute-start | bytes 78956 | tf_op jit(solution)/shard_map/ppermute | solution.py:29
  661.8 6.2 collective-permute-start.18
  670.8 10.6 %collective-permute-start.19 = (f32[3,19,19,1]{2,1,3,0:T(8,128)S(1)}, f32[3,19,19,1]{2,1,3,0:T(8,128)S(1)}, u32[]{:S(2)}, u32[]{:S(2)}) collective-permute-start(f32[3,19,19,1]{2,1,3,0:T(8,128)S(1)} %copy.56), channel_id=1, source_target_pairs={{0,1},{1,2},{2,3},{4,5},{5,6},{6,7},{8,9},{9,10},{10,11},{12,13},{... | collective-permute-start | bytes 13004 | tf_op jit(solution)/shard_map/ppermute | solution.py:26
  677.0 5.0 collective-permute-start.20
  763.2 107.4 %collective-permute-start.21 = (f32[2,16,128]{2,1,0:T(8,128)S(1)}, f32[2,16,128]{2,1,0:T(8,128)S(1)}, u32[]{:S(2)}, u32[]{:S(2)}) collective-permute-start(f32[2,16,128]{2,1,0:T(8,128)S(1)} %get-tuple-element.615), channel_id=1, source_target_pairs={{0,32},{32,64},{64,96},{96,128},{128,160},{160,192},{192,224},{1,3... | collective-permute-start | bytes 49160 | tf_op jit(solution)/shard_map/ppermute | solution.py:26
  844.4 27.1 %collective-permute-start.22 = (f32[2,16,128]{2,1,0:T(8,128)S(1)}, f32[2,16,128]{2,1,0:T(8,128)S(1)}, u32[]{:S(2)}, u32[]{:S(2)}) collective-permute-start(f32[2,16,128]{2,1,0:T(8,128)S(1)} %get-tuple-element.616), channel_id=1, source_target_pairs={{32,0},{64,32},{96,64},{128,96},{160,128},{192,160},{224,192},{33,... | collective-permute-start | bytes 49160 | tf_op jit(solution)/shard_map/ppermute | solution.py:29
  872.8 4.5 collective-permute-start.24
  877.5 11.1 %collective-permute-start.25 = (f32[20,20,2]{2,1,0:T(8,128)S(1)}, f32[20,20,2]{2,1,0:T(8,128)S(1)}, u32[]{:S(2)}, u32[]{:S(2)}) collective-permute-start(f32[20,20,2]{2,1,0:T(8,128)S(1)} %get-tuple-element.601), channel_id=1, source_target_pairs={{0,1},{1,2},{2,3},{4,5},{5,6},{6,7},{8,9},{9,10},{10,11},{12,13},{... | collective-permute-start | bytes 9608 | tf_op jit(solution)/shard_map/ppermute | solution.py:26
  883.2 9.7 %collective-permute-start.26 = (f32[20,20,2]{2,1,0:T(8,128)S(1)}, f32[20,20,2]{2,1,0:T(8,128)S(1)}, u32[]{:S(2)}, u32[]{:S(2)}) collective-permute-start(f32[20,20,2]{2,1,0:T(8,128)S(1)} %get-tuple-element.602), channel_id=1, source_target_pairs={{1,0},{2,1},{3,2},{5,4},{6,5},{7,6},{9,8},{10,9},{11,10},{13,12},{... | collective-permute-start | bytes 9608 | tf_op jit(solution)/shard_map/ppermute | solution.py:29
  (72 other events, 1794.7 us)
where the time goes:
time: 908 us; the launch traced here: 897 us
  starting transfers between devices  602 us (66%)
  local copies, waits for them, and re-layouts  131 us (14%)
  blocking collectives  69.8 us (8%)
  waiting for transfers between devices  38.3 us (4%)
  other arithmetic  28.5 us (3%)
  loops' own time  16.8 us (2%)
    ppermute x12, starting transfers between devices, with_halo(): lax.ppermute(lax.slice_in_dim(block, block.shape[dim] - width, None, axis...  446 us
    ppermute x12, starting transfers between devices, with_halo(): lax.ppermute(lax.slice_in_dim(block, 0, width, axis=dim), axis, backward)  150 us
    psum x8, blocking collectives, over_axes(): value = lax.psum(value, axis)  69.8 us
    ppermute x12, waiting for transfers between devices, with_halo(): lax.ppermute(lax.slice_in_dim(block, 0, width, axis=dim), axis, backward)  24.8 us
    dynamic_update_slice x2, local copies, waits for them, and re-layouts, add_into(): lax.dynamic_update_slice_in_dim(summed, current + contribution, offset_z, 3)  22.9 us
    dynamic_slice x16, local copies, waits for them, and re-layouts, brick_step(): return lax.cond(own_flags[position] > 0, brick_compute, skip_brick, summed)  20.1 us
    cond x27, local copies, waits for them, and re-layouts  19.4 us
  transfers between devices with their start and end apart: 27, of which 13 were waited for; matrix products, arithmetic and copies ran while one was open for 2% of the time, Pallas kernels for 0%

commit v1 on v0

--- a/solution.py
+++ b/solution.py
@@ -18,6 +18,11 @@
 precise = lax.Precision.HIGHEST
 
 
+def compute_tails_over_axis(array_in, bus_axis):
+    val = lax.all_gather(array_in, bus_axis).sum(axis=0)
+    return val
+
+
 def with_halo(block, sides, width):
     for axis, dim in sides:
         count = lax.axis_size(axis)
@@ -39,7 +44,7 @@
 
 def over_axes(value, axes):
     for axis in axes:
-        value = lax.psum(value, axis)
+        value = compute_tails_over_axis(value, axis)
     return value
 
 

time: 908 us -> 946 us (1.042)
  local copies, waits for them, and re-layouts: 131 us -> 154 us
  starting transfers between devices: 602 us -> 613 us
  other arithmetic: 28.5 us -> 38.4 us
    psum x8 -> x0, blocking collectives: 69.8 us -> none  [over_axes(): value = lax.psum(value, axis)]
    unnamed x0 -> x8, blocking collectives: none -> 64.3 us
    unnamed x135 -> x179, local copies, waits for them, and re-layouts: 3.45 us -> 27.2 us
    ppermute x12, starting transfers between devices: 446 us -> 457 us  [with_halo(): lax.ppermute(lax.slice_in_dim(block, block.shape[dim] - width, None, axis...]
    reduce_sum x0 -> x16, other arithmetic: none -> 9.91 us  [compute_tails_over_axis(): val = lax.all_gather(array_in, bus_axis).sum(axis=0)]
  transfers between devices with their start and end apart: 27 -> 27, of which waited for: 13 -> 12; matrix products, arithmetic and copies ran while one was open for 2% -> 2% of each run, Pallas kernels for 0% -> 0%
where the time goes in v1:
time: 946 us; the launch traced here: 934 us
  starting transfers between devices  613 us (65%)
  local copies, waits for them, and re-layouts  154 us (16%)
  blocking collectives  64.3 us (7%)
  other arithmetic  38.4 us (4%)
  waiting for transfers between devices  37.6 us (4%)
  loops' own time  16.8 us (2%)
    ppermute x12, starting transfers between devices, with_halo(): lax.ppermute(lax.slice_in_dim(block, block.shape[dim] - width, None, axis...  457 us
    ppermute x12, starting transfers between devices, with_halo(): lax.ppermute(lax.slice_in_dim(block, 0, width, axis=dim), axis, backward)  150 us
    unnamed x8, blocking collectives  64.3 us
    unnamed x179, local copies, waits for them, and re-layouts  27.2 us
    ppermute x12, waiting for transfers between devices, with_halo(): lax.ppermute(lax.slice_in_dim(block, 0, width, axis=dim), axis, backward)  24 us
    dynamic_update_slice x2, local copies, waits for them, and re-layouts, add_into(): lax.dynamic_update_slice_in_dim(summed, current + contribution, offset_z, 3)  22.9 us
    cond x27, local copies, waits for them, and re-layouts  19.5 us
    dynamic_slice x16, local copies, waits for them, and re-layouts, brick_step(): return lax.cond(own_flags[position] > 0, brick_compute, skip_brick, summed)  19.3 us
  transfers between devices with their start and end apart: 27, of which 12 were waited for; matrix products, arithmetic and copies ran while one was open for 2% of the time, Pallas kernels for 0%

profile of v1, /device:TPU:1, one launch (start us, length us, event | category | flops | bytes accessed | tf_op | source)
XLA Modules:
  0.0 934.0 jit_solution(12375417718896192266)
XLA Ops:
  12.2 8.5 collective-permute-done
  48.3 46.5 %while.51 = (s32[]{:T(128)}, f32[3,17,17,129]{3,2,1,0:T(8,128)}, s32[8]{0:T(128)}, f32[3,17,17,129]{3,2,1,0:T(8,128)S(1)}, f32[16,16,128]{2,1,0:T(8,128)}, /*index=5*/s32[]{:T(128)}, s32[1]{0:T(128)}) while((s32[]{:T(128)}, f32[3,17,17,129]{3,2,1,0:T(8,128)}, s32[8]{0:T(128)}, f32[3,17,17,129]{3,2,1,0:T(8,128)S(1)}, ...), condition=%wide.region_8.9_spmd.clone, body=%wide.region_5.8_spmd.sunk.clone.sunk | while | flops 28527780 | bytes 7407486 | solution.py:257
  55.8 31.4 %conditional.12 = (f32[3,17,17,129]{3,2,1,0:T(8,128)}) conditional(s32[]{:T(128)} %bitcast.53, f32[3,17,17,129]{3,2,1,0:T(8,128)} %get-tuple-element.762, (s32[]{:T(128)}, f32[3,17,17,129]{3,2,1,0:T(8,128)}, f32[3,17,17,129]{3,2,1,0:T(8,128)S(1)}, f32[16,16,128]{2,1,0:T(8,128)}) %tuple.222), branch_computations={%region_6.6_spmd, %region_7.7_spmd.clone} | conditional | flops 28527776 | bytes 7407351 | solution.py:255
  75.8 11.4 %dynamic_update_slice.12 = f32[3,17,17,129]{3,2,1,0:T(8,128)} dynamic-update-slice(f32[3,17,17,129]{3,2,1,0:T(8,128)} %get-tuple-element.486, f32[3,17,17,17]{3,2,1,0:T(8,128)S(1)} %add_add_fusion, s32[]{:T(128)} %constant.166.clone.1, s32[]{:T(128)} %constant.166.clone.1, s32[]{:T(128)} %constant.166.clone.1, s32[]{:T(128)S(6)} %select_n.81) | dynamic-update-slice | bytes 117916 | tf_op jit(solution)/shard_map/while/body/eval_jaxpr/cond/branch_1_fun/dynamic_update_slice | solution.py:238
  95.7 163.3 %collective-permute-start.9 = (f32[3,1,17,129]{3,2,1,0:T(8,128)S(1)}, f32[3,1,17,129]{3,2,1,0:T(8,128)S(1)}, u32[]{:S(2)}, u32[]{:S(2)}) collective-permute-start(f32[3,1,17,129]{3,2,1,0:T(8,128)S(1)} %get-tuple-element.599), channel_id=1, source_target_pairs={{0,32},{32,64},{64,96},{96,128},{128,160},{160,192},{192,224},{1,3... | collective-permute-start | bytes 78956 | tf_op jit(solution)/shard_map/ppermute | solution.py:31
  259.1 54.8 %collective-permute-start.10 = (f32[3,1,17,129]{3,2,1,0:T(8,128)S(1)}, f32[3,1,17,129]{3,2,1,0:T(8,128)S(1)}, u32[]{:S(2)}, u32[]{:S(2)}) collective-permute-start(f32[3,1,17,129]{3,2,1,0:T(8,128)S(1)} %get-tuple-element.600), channel_id=1, source_target_pairs={{32,0},{64,32},{96,64},{128,96},{160,128},{192,160},{224,192},{33,... | collective-permute-start | bytes 78956 | tf_op jit(solution)/shard_map/ppermute | solution.py:34
  326.1 21.4 %collective-permute-start.13 = (f32[3,19,19,1]{2,1,3,0:T(8,128)S(1)}, f32[3,19,19,1]{2,1,3,0:T(8,128)S(1)}, u32[]{:S(2)}, u32[]{:S(2)}) collective-permute-start(f32[3,19,19,1]{2,1,3,0:T(8,128)S(1)} %copy.48), channel_id=1, source_target_pairs={{0,1},{1,2},{2,3},{4,5},{5,6},{6,7},{8,9},{9,10},{10,11},{12,13},{... | collective-permute-start | bytes 13004 | tf_op jit(solution)/shard_map/ppermute | solution.py:31
  365.0 6.0 all-reduce.37
  375.5 6.8 all-reduce.39
  386.7 12.4 %all-reduce.33 = (f32[8]{0:T(128)S(1)}, f32[8]{0:T(128)S(1)}) all-reduce(f32[8]{0:T(128)S(1)} %dynamic-update-slice.2, f32[8]{0:T(128)S(1)} %dynamic-update-slice.6), channel_id=1, replica_groups=mesh['gx_0'=4,'gx_1'=2,'gy'=8,'gz'=4] {'gy'}, use_global_device_ids=true, to_apply=%add.18 | all-reduce | flops 16 | bytes 128
  403.1 6.0 all-reduce.35
  414.3 46.4 %while.52 = (s32[]{:T(128)}, f32[3,17,17,129]{3,2,1,0:T(8,128)}, s32[8]{0:T(128)}, f32[3,17,17,129]{3,2,1,0:T(8,128)S(1)}, f32[16,16,128]{2,1,0:T(8,128)}, /*index=5*/s32[]{:T(128)}, s32[1]{0:T(128)}) while((s32[]{:T(128)}, f32[3,17,17,129]{3,2,1,0:T(8,128)}, s32[8]{0:T(128)}, f32[3,17,17,129]{3,2,1,0:T(8,128)S(1)}, ...), condition=%wide.region_22.23_spmd.clone, body=%wide.region_19.22_spmd.sunk.clone.sunk | while | flops 28527780 | bytes 7407486 | solution.py:257
  421.8 31.3 %conditional.13 = (f32[3,17,17,129]{3,2,1,0:T(8,128)}) conditional(s32[]{:T(128)} %bitcast.54, f32[3,17,17,129]{3,2,1,0:T(8,128)} %get-tuple-element.783, (s32[]{:T(128)}, f32[3,17,17,129]{3,2,1,0:T(8,128)}, f32[3,17,17,129]{3,2,1,0:T(8,128)S(1)}, f32[16,16,128]{2,1,0:T(8,128)}) %tuple.224), branch_computations={%region_20.20_spmd, %region_21.21_spmd.clone} | conditional | flops 28527776 | bytes 7407351 | solution.py:255
  441.7 11.4 %dynamic_update_slice.13 = f32[3,17,17,129]{3,2,1,0:T(8,128)} dynamic-update-slice(f32[3,17,17,129]{3,2,1,0:T(8,128)} %get-tuple-element.494, f32[3,17,17,17]{3,2,1,0:T(8,128)S(1)} %add_add_fusion.1, s32[]{:T(128)} %constant.174.clone.1, s32[]{:T(128)} %constant.174.clone.1, s32[]{:T(128)} %constant.174.clone.1, s32[]{:T(128)S(6)} %select_n.83) | dynamic-update-slice | bytes 117916 | tf_op jit(solution)/shard_map/while/body/eval_jaxpr/cond/branch_1_fun/dynamic_update_slice | solution.py:238
  461.7 165.3 %collective-permute-start.15 = (f32[3,1,17,129]{3,2,1,0:T(8,128)S(1)}, f32[3,1,17,129]{3,2,1,0:T(8,128)S(1)}, u32[]{:S(2)}, u32[]{:S(2)}) collective-permute-start(f32[3,1,17,129]{3,2,1,0:T(8,128)S(1)} %get-tuple-element.593), channel_id=1, source_target_pairs={{0,32},{32,64},{64,96},{96,128},{128,160},{160,192},{192,224},{1,3... | collective-permute-start | bytes 78956 | tf_op jit(solution)/shard_map/ppermute | solution.py:31
  627.0 56.4 %collective-permute-start.16 = (f32[3,1,17,129]{3,2,1,0:T(8,128)S(1)}, f32[3,1,17,129]{3,2,1,0:T(8,128)S(1)}, u32[]{:S(2)}, u32[]{:S(2)}) collective-permute-start(f32[3,1,17,129]{3,2,1,0:T(8,128)S(1)} %get-tuple-element.594), channel_id=1, source_target_pairs={{32,0},{64,32},{96,64},{128,96},{160,128},{192,160},{224,192},{33,... | collective-permute-start | bytes 78956 | tf_op jit(solution)/shard_map/ppermute | solution.py:34
  716.4 6.7 all-reduce.36
  727.0 6.4 all-reduce.38
  737.2 12.1 %all-reduce.32 = (f32[8]{0:T(128)S(1)}, f32[8]{0:T(128)S(1)}) all-reduce(f32[8]{0:T(128)S(1)} %dynamic-update-slice.10, f32[8]{0:T(128)S(1)} %dynamic-update-slice.14), channel_id=1, replica_groups=mesh['gx_0'=4,'gx_1'=2,'gy'=8,'gz'=4] {'gy'}, use_global_device_ids=true, to_apply=%add.26 | all-reduce | flops 16 | bytes 128
  753.3 8.0 all-reduce.34
  768.8 29.5 %while.53 = (s32[]{:T(128)}, f32[16,16,128]{2,1,0:T(8,128)S(1)}, s32[8]{0:T(128)}, f32[3,17,17,129]{3,2,1,0:T(8,128)S(1)}, s32[]{:T(128)}, /*index=5*/s32[1]{0:T(128)}) while((s32[]{:T(128)}, f32[16,16,128]{2,1,0:T(8,128)S(1)}, s32[8]{0:T(128)}, f32[3,17,17,129]{3,2,1,0:T(8,128)S(1)}, s32[]{:T(128)}, ...), condition=%wide.region_32.33_spmd.clone, body=%wide.region_28.32_spmd.sunk.clone.sunk | while | flops 28504076 | bytes 4812342 | solution.py:306
  776.4 14.4 %conditional.14 = (f32[16,16,128]{2,1,0:T(8,128)S(1)}) conditional(s32[]{:T(128)} %bitcast.55, f32[16,16,128]{2,1,0:T(8,128)S(1)} %get-tuple-element.803, (s32[]{:T(128)}, f32[3,17,17,129]{3,2,1,0:T(8,128)S(1)}, f32[16,16,128]{2,1,0:T(8,128)S(1)}) %tuple.226), branch_computations={%region_29.29_spmd, %region_30.31_spmd.clone} | conditional | flops 28504072 | bytes 4812223 | solution.py:304
  800.3 81.5 %collective-permute-start.21 = (f32[2,16,128]{2,1,0:T(8,128)S(1)}, f32[2,16,128]{2,1,0:T(8,128)S(1)}, u32[]{:S(2)}, u32[]{:S(2)}) collective-permute-start(f32[2,16,128]{2,1,0:T(8,128)S(1)} %get-tuple-element.615), channel_id=1, source_target_pairs={{0,32},{32,64},{64,96},{96,128},{128,160},{160,192},{192,224},{1,3... | collective-permute-start | bytes 49160 | tf_op jit(solution)/shard_map/ppermute | solution.py:31
  881.8 26.3 %collective-permute-start.22 = (f32[2,16,128]{2,1,0:T(8,128)S(1)}, f32[2,16,128]{2,1,0:T(8,128)S(1)}, u32[]{:S(2)}, u32[]{:S(2)}) collective-permute-start(f32[2,16,128]{2,1,0:T(8,128)S(1)} %get-tuple-element.616), channel_id=1, source_target_pairs={{32,0},{64,32},{96,64},{128,96},{160,128},{192,160},{224,192},{33,... | collective-permute-start | bytes 49160 | tf_op jit(solution)/shard_map/ppermute | solution.py:34
  (438 shorter events, 244.0 us)
Async XLA Ops:
  1.4 20.7 %collective-permute-start.3 = (f32[2,16,128]{2,1,0:T(8,128)S(1)}, f32[2,16,128]{2,1,0:T(8,128)S(1)}, u32[]{:S(2)}, u32[]{:S(2)}) collective-permute-start(f32[2,16,128]{2,1,0:T(8,128)S(1)} %get-tuple-element.621), channel_id=1, source_target_pairs={{0,32},{32,64},{64,96},{96,128},{128,160},{160,192},{192,224},{1,3... | collective-permute-start | bytes 49160 | tf_op jit(solution)/shard_map/ppermute | solution.py:31
  5.9 16.3 %collective-permute-start.4 = (f32[2,16,128]{2,1,0:T(8,128)S(1)}, f32[2,16,128]{2,1,0:T(8,128)S(1)}, u32[]{:S(2)}, u32[]{:S(2)}) collective-permute-start(f32[2,16,128]{2,1,0:T(8,128)S(1)} %get-tuple-element.620), channel_id=1, source_target_pairs={{32,0},{64,32},{96,64},{128,96},{160,128},{192,160},{224,192},{33,... | collective-permute-start | bytes 49160 | tf_op jit(solution)/shard_map/ppermute | solution.py:34
  7.8 12.9 %collective-permute-start = (f32[3,16,16,1]{3,2,1,0:T(8,128)}, f32[3,16,16,1]{3,2,1,0:T(8,128)S(1)}, u32[]{:S(2)}, u32[]{:S(2)}) collective-permute-start(f32[3,16,16,1]{3,2,1,0:T(8,128)} %bitcast.56), channel_id=1, source_target_pairs={{1,0},{2,1},{3,2},{5,4},{6,5},{7,6},{9,8},{10,9},{11,10},{13,12},{... | collective-permute-start | bytes 9224 | tf_op jit(solution)/shard_map/ppermute | solution.py:42
  20.8 6.9 collective-permute-start.1
  22.2 5.5 collective-permute-start.5
  26.2 4.5 collective-permute-start.6
  30.9 6.9 collective-permute-start.7
  33.1 8.2 collective-permute-start.8
  34.4 12.1 %collective-permute-start.2 = (f32[3,1,17,129]{3,2,1,0:T(8,128)S(1)}, f32[3,1,17,129]{3,2,1,0:T(8,128)S(1)}, u32[]{:S(2)}, u32[]{:S(2)}) collective-permute-start(f32[3,1,17,129]{3,2,1,0:T(8,128)S(1)} %pad_maximum_fusion.25), channel_id=1, source_target_pairs={{32,0},{64,32},{96,64},{128,96},{160,128},{192,160},{224,192},{33,... | collective-permute-start | bytes 78956 | tf_op jit(solution)/shard_map/ppermute | solution.py:42
  95.7 219.8 %collective-permute-start.9 = (f32[3,1,17,129]{3,2,1,0:T(8,128)S(1)}, f32[3,1,17,129]{3,2,1,0:T(8,128)S(1)}, u32[]{:S(2)}, u32[]{:S(2)}) collective-permute-start(f32[3,1,17,129]{3,2,1,0:T(8,128)S(1)} %get-tuple-element.599), channel_id=1, source_target_pairs={{0,32},{32,64},{64,96},{96,128},{128,160},{160,192},{192,224},{1,3... | collective-permute-start | bytes 78956 | tf_op jit(solution)/shard_map/ppermute | solution.py:31
  259.1 56.5 %collective-permute-start.10 = (f32[3,1,17,129]{3,2,1,0:T(8,128)S(1)}, f32[3,1,17,129]{3,2,1,0:T(8,128)S(1)}, u32[]{:S(2)}, u32[]{:S(2)}) collective-permute-start(f32[3,1,17,129]{3,2,1,0:T(8,128)S(1)} %get-tuple-element.600), channel_id=1, source_target_pairs={{32,0},{64,32},{96,64},{128,96},{160,128},{192,160},{224,192},{33,... | collective-permute-start | bytes 78956 | tf_op jit(solution)/shard_map/ppermute | solution.py:34
  317.0 6.2 collective-permute-start.12
  326.1 25.9 %collective-permute-start.13 = (f32[3,19,19,1]{2,1,3,0:T(8,128)S(1)}, f32[3,19,19,1]{2,1,3,0:T(8,128)S(1)}, u32[]{:S(2)}, u32[]{:S(2)}) collective-permute-start(f32[3,19,19,1]{2,1,3,0:T(8,128)S(1)} %copy.48), channel_id=1, source_target_pairs={{0,1},{1,2},{2,3},{4,5},{5,6},{6,7},{8,9},{9,10},{10,11},{12,13},{... | collective-permute-start | bytes 13004 | tf_op jit(solution)/shard_map/ppermute | solution.py:31
  348.6 5.0 collective-permute-start.14
  461.7 223.4 %collective-permute-start.15 = (f32[3,1,17,129]{3,2,1,0:T(8,128)S(1)}, f32[3,1,17,129]{3,2,1,0:T(8,128)S(1)}, u32[]{:S(2)}, u32[]{:S(2)}) collective-permute-start(f32[3,1,17,129]{3,2,1,0:T(8,128)S(1)} %get-tuple-element.593), channel_id=1, source_target_pairs={{0,32},{32,64},{64,96},{96,128},{128,160},{160,192},{192,224},{1,3... | collective-permute-start | bytes 78956 | tf_op jit(solution)/shard_map/ppermute | solution.py:31
  627.0 58.1 %collective-permute-start.16 = (f32[3,1,17,129]{3,2,1,0:T(8,128)S(1)}, f32[3,1,17,129]{3,2,1,0:T(8,128)S(1)}, u32[]{:S(2)}, u32[]{:S(2)}) collective-permute-start(f32[3,1,17,129]{3,2,1,0:T(8,128)S(1)} %get-tuple-element.594), channel_id=1, source_target_pairs={{32,0},{64,32},{96,64},{128,96},{160,128},{192,160},{224,192},{33,... | collective-permute-start | bytes 78956 | tf_op jit(solution)/shard_map/ppermute | solution.py:34
  686.5 6.2 collective-permute-start.18
  695.6 10.6 %collective-permute-start.19 = (f32[3,19,19,1]{2,1,3,0:T(8,128)S(1)}, f32[3,19,19,1]{2,1,3,0:T(8,128)S(1)}, u32[]{:S(2)}, u32[]{:S(2)}) collective-permute-start(f32[3,19,19,1]{2,1,3,0:T(8,128)S(1)} %copy.56), channel_id=1, source_target_pairs={{0,1},{1,2},{2,3},{4,5},{5,6},{6,7},{8,9},{9,10},{10,11},{12,13},{... | collective-permute-start | bytes 13004 | tf_op jit(solution)/shard_map/ppermute | solution.py:31
  701.7 5.0 collective-permute-start.20
  800.3 107.8 %collective-permute-start.21 = (f32[2,16,128]{2,1,0:T(8,128)S(1)}, f32[2,16,128]{2,1,0:T(8,128)S(1)}, u32[]{:S(2)}, u32[]{:S(2)}) collective-permute-start(f32[2,16,128]{2,1,0:T(8,128)S(1)} %get-tuple-element.615), channel_id=1, source_target_pairs={{0,32},{32,64},{64,96},{96,128},{128,160},{160,192},{192,224},{1,3... | collective-permute-start | bytes 49160 | tf_op jit(solution)/shard_map/ppermute | solution.py:31
  881.8 27.1 %collective-permute-start.22 = (f32[2,16,128]{2,1,0:T(8,128)S(1)}, f32[2,16,128]{2,1,0:T(8,128)S(1)}, u32[]{:S(2)}, u32[]{:S(2)}) collective-permute-start(f32[2,16,128]{2,1,0:T(8,128)S(1)} %get-tuple-element.616), channel_id=1, source_target_pairs={{32,0},{64,32},{96,64},{128,96},{160,128},{192,160},{224,192},{33,... | collective-permute-start | bytes 49160 | tf_op jit(solution)/shard_map/ppermute | solution.py:34
  910.3 4.5 collective-permute-start.24
  915.0 11.1 %collective-permute-start.25 = (f32[20,20,2]{2,1,0:T(8,128)S(1)}, f32[20,20,2]{2,1,0:T(8,128)S(1)}, u32[]{:S(2)}, u32[]{:S(2)}) collective-permute-start(f32[20,20,2]{2,1,0:T(8,128)S(1)} %get-tuple-element.601), channel_id=1, source_target_pairs={{0,1},{1,2},{2,3},{4,5},{5,6},{6,7},{8,9},{9,10},{10,11},{12,13},{... | collective-permute-start | bytes 9608 | tf_op jit(solution)/shard_map/ppermute | solution.py:31
  920.7 9.7 %collective-permute-start.26 = (f32[20,20,2]{2,1,0:T(8,128)S(1)}, f32[20,20,2]{2,1,0:T(8,128)S(1)}, u32[]{:S(2)}, u32[]{:S(2)}) collective-permute-start(f32[20,20,2]{2,1,0:T(8,128)S(1)} %get-tuple-element.602), channel_id=1, source_target_pairs={{1,0},{2,1},{3,2},{5,4},{6,5},{7,6},{9,8},{10,9},{11,10},{13,12},{... | collective-permute-start | bytes 9608 | tf_op jit(solution)/shard_map/ppermute | solution.py:34
  (76 other events, 1905.5 us)
